TPU v7x, 32 devices: a whole 2x2x4 slice. The times are simulated.
32 devices in a mesh: groups: 2 (over y), tok: 4 (over z), head: 4 (over x, core).
Axes of the slice: x: 2, y: 2, z: 4, core: 2. Of those that a mesh axis runs over, the one named last changes fastest.
Arguments:
- hidden: bfloat16 [2560, 8192], P(('groups', 'tok'), 'head'), parts along dimension 0, may hold values from -6 to 6
- positions: int32 [2560], P(('groups', 'tok')), parts along dimension 0, may hold values from 0 to 1279, as said below
- norm_gain: float32 [8192], P('head'), may hold values from 0.1 to 1.9
- w_key: bfloat16 [8192, 1024], P('head'), may hold values from -0.0625 to 0.0625
- w_value: bfloat16 [8192, 1024], P('head'), may hold values from -0.0625 to 0.0625
- queries: bfloat16 [512, 8192], P(('groups', 'tok'), 'head'), parts along dimension 0, may hold values from -400 to 400
- lengths: int32 [512], P(('groups', 'tok')), parts along dimension 0, may hold values from 1 to 1280
Outputs:
- attended: bfloat16 [512, 8192], P(('groups', 'tok'), 'head'), parts along dimension 0
There are 2 independent parts, one for each index of `groups`. A program takes and returns all parts, laid end to end along the dimension named above; an argument that names none is the same for every part. Nothing has to cross between parts.
Inputs may be any that keep to these rules, and one draw needn't show every extreme that they name: `positions`: each of 0 to 1279 appears once.
All inputs are finite; a program needn't handle non-finite values.
Results may differ from a plain program's by a relative error of at most 0.025.
The roundings to bfloat16 on the way count: a program that leaves them out, or rounds other values in their place, can miss the bound.
Values may be sent and summed in bfloat16 or wider, within the bound.
A program may use at most 64 MiB of HBM per device.

v0:
```python
import jax
import jax.numpy as jnp
from jax import lax
from jax.sharding import PartitionSpec as P

HD = 128
QPK = 8


def rotate_columns(keys_t, positions):
    half = keys_t.shape[1] // 2
    width = keys_t.shape[1]
    freq = 500000.0 ** (-(jnp.arange(half, dtype=jnp.float32) * 2.0) / width)
    angle = positions.astype(jnp.float32)[None, :] * freq[:, None]
    cosine = jnp.cos(angle)[None]
    sine = jnp.sin(angle)[None]
    first = keys_t[:, :half]
    second = keys_t[:, half:]
    return jnp.concatenate([first * cosine - second * sine, second * cosine + first * sine], axis=1)


def project_columns(weight_rows, normed_piece):
    return lax.dot_general(
        weight_rows, normed_piece, (((0,), (1,)), ((), ())), preferred_element_type=jnp.float32
    )


def body(hidden, positions, norm_gain, w_key, w_value, queries, lengths):
    tok_rows = hidden.shape[0]
    full_width = hidden.shape[1] * lax.axis_size("head")
    kv_here = w_key.shape[1] // HD // lax.axis_size("head")
    wide = hidden.astype(jnp.float32)
    squares = lax.psum(jnp.sum(wide * wide, axis=1), "head")
    normed = (wide * lax.rsqrt(squares / full_width + 1e-05)[:, None] * norm_gain).astype(
        jnp.bfloat16
    )
    query_all, length_all = (
        lax.all_gather(queries, "tok", axis=0, tiled=True),
        lax.all_gather(lengths, "tok", axis=0, tiled=True),
    )
    stride = 2 * HD
    heads = kv_here * stride * lax.axis_size("head") // stride
    key_term = project_columns(w_key, normed).reshape(heads, HD, tok_rows)
    value_term = project_columns(w_value, normed).reshape(heads, HD, tok_rows)
    summed = lax.psum_scatter(
        jnp.stack((key_term, value_term), axis=1).reshape(heads * stride, tok_rows),
        "head",
        scatter_dimension=0,
        tiled=True,
    )
    summed = summed.reshape(kv_here, 2, HD, tok_rows)
    key_t = summed[:, 0]
    value_t = summed[:, 1]
    keys_t = rotate_columns(key_t, positions).astype(jnp.bfloat16)
    values_t = value_t.astype(jnp.bfloat16)
    row_total = query_all.shape[0]
    grouped = query_all.reshape(row_total, kv_here, QPK, HD)
    scores = jnp.einsum(
        "rjgd,jdp->jrgp", grouped, keys_t, preferred_element_type=jnp.float32
    ) * HD ** (-0.5)
    valid = positions[None, :] < length_all[:, None]
    scores = jnp.where(valid[None, :, None, :], scores, -1e30)
    top = lax.pmax(jnp.max(scores, axis=3), "tok")
    weights = jnp.exp(scores - top[..., None]).astype(jnp.bfloat16)
    numer = jnp.einsum("jrgp,jdp->rjgd", weights, values_t, preferred_element_type=jnp.float32)
    numer = numer.reshape(row_total, kv_here * QPK * HD)
    denom = (
        jnp.sum(weights.astype(jnp.float32), axis=3)
        .transpose(1, 0, 2)
        .reshape(row_total, kv_here * QPK)
    )
    own_rows = row_total // lax.axis_size("tok")
    numer_all, denom_all = lax.psum((numer, denom), "tok")
    offset = lax.axis_index("tok") * own_rows
    numer_mine = lax.dynamic_slice_in_dim(numer_all, offset, own_rows, 0)
    denom_mine = lax.dynamic_slice_in_dim(denom_all, offset, own_rows, 0)
    result = numer_mine.reshape(own_rows, kv_here * QPK, HD) / denom_mine[..., None]
    return result.reshape(own_rows, kv_here * QPK * HD).astype(jnp.bfloat16)


def solution(mesh):
    in_specs = (
        P(("groups", "tok"), "head"),
        P(("groups", "tok")),
        P("head"),
        P("head", None),
        P("head", None),
        P(("groups", "tok"), "head"),
        P(("groups", "tok")),
    )
    out_specs = P(("groups", "tok"), "head")
    return jax.shard_map(body, mesh=mesh, in_specs=in_specs, out_specs=out_specs, check_vma=False)
```

profile of v0, /device:TPU:0, one launch (start us, length us, event | category | flops | bytes accessed | tf_op | source)
XLA Modules:
  0.0 189.0 jit_solution(3143006847289780138)
XLA Ops:
  7.4 0.0 all-gather.2.cloned.1.call-start
  7.4 0.7 all-gather.2.cloned.1.call-update
  8.1 0.0 reduce-scatter.2.cloned.1.call-start
  8.1 1.7 fusion.1
  9.8 8.4 %psum.21 = f32[320]{0:T(512)S(1)} all-reduce(f32[320]{0:T(512)S(1)} %fusion.1), channel_id=1, replica_groups=mesh['groups'=2,'tok'=4,'head'=4] {'head'}, use_global_device_ids=true, to_apply=%region_1.0 | all-reduce | flops 320 | bytes 2560 | tf_op jit(solution)/shard_map/psum | solution.py:33
  18.2 0.0 copy-start
  18.2 0.0 copy-start.2
  18.2 0.0 copy-start.3
  18.2 4.5 %convolution_bitcast_fusion = f32[40,8,8,128]{3,1,2,0:T(8,128)S(1)} fusion(bf16[2048,1024]{1,0:T(8,128)(2,1)} %param.11, bf16[320,2048]{1,0:T(8,128)(2,1)} %param.7, f32[2048]{0:T(1024)} %param.9, f32[320]{0:T(512)S(1)} %add_rsqrt_fusion), kind=kOutput, calls=%fused_computation.10 | convolution fusion | flops 1344798720 | bytes 6825216 | tf_op jit(solution)/shard_map/dot_general | solution.py:23
  22.7 0.3 copy.31
  23.0 0.0 copy-done
  23.0 0.0 copy-done.2
  23.0 0.0 copy-done.3
  23.0 1.6 convolution_bitcast_fusion.1
  24.6 0.3 copy.30
  24.9 2.4 %pad_maximum_fusion = f32[8,2,128,320]{2,1,0,3:T(2,128)S(1)} fusion(f32[8,1,128,320]{2,1,0,3:T(1,128)S(1)} %bitcast.64, f32[8,1,128,320]{2,1,0,3:T(1,128)S(1)} %bitcast.65), kind=kLoop, calls=%fused_computation.9 | loop fusion | flops 655360 | bytes 5242880 | tf_op jit(solution)/shard_map/stack | solution.py:46
  27.2 3.2 %reshape.111 = f32[2048,320]{0,1:T(8,128)} reshape(f32[8,2,128,320]{2,1,0,3:T(2,128)S(1)} %pad_maximum_fusion) | data formatting | bytes 5242880 | tf_op jit(solution)/shard_map/reshape | solution.py:46
  30.4 0.0 copy-start.1
  30.4 0.0 copy-start.5
  30.5 0.0 reduce-scatter.2.cloned.1.call-update
  30.5 0.0 all-reduce.3.cloned.1.call-start
  30.5 0.6 copy-done.1
  31.1 0.0 copy-done.5
  31.1 0.6 dynamic-slice
  32.4 0.0 copy-done.4
  32.4 0.2 dynamic-update-slice
  32.6 8.6 %all-reduce = s32[256]{0:T(256)S(1)} all-reduce(s32[256]{0:T(256)S(1)} %dynamic-update-slice), channel_id=1, replica_groups=mesh['groups'=2,'tok'=4,'head'=4] {'tok'}, use_global_device_ids=true, to_apply=%add | all-reduce | flops 256 | bytes 2048
  41.3 0.1 broadcast_compare_fusion
  41.4 0.6 multiply_cosine_fusion
  42.0 0.0 all-gather.2.cloned.1.call-done
  42.1 1.5 copy.21
  43.6 21.7 %reduce-scatter.2.cloned.1.call-done = f32[512,320]{0,1:T(8,128)} async-done(((f32[2048,320]{0,1:T(8,128)}), f32[512,320]{0,1:T(8,128)}) %reduce-scatter.2.cloned.1.call-update) | async-done | bytes 655376 | tf_op jit(solution)/shard_map/reduce_scatter | solution.py:45
  65.2 1.5 reshape.112
  66.7 0.3 slice.17
  67.1 0.2 slice.18
  67.4 0.2 subtract_convert_fusion
  67.5 3.3 %fusion = (f32[2,256,8]{1,2,0:T(8,128)S(1)}, f32[2,320,256,8]{2,1,3,0:T(8,128)}) fusion(pred[256,320]{0,1:T(8,128)(4,1)S(1)} %broadcast_compare_fusion, bf16[256,2,8,128]{0,3,2,1:T(8,128)(2,1)S(1)} %bitcast.66, bf16[2,64,320]{1,2,0:T(8,128)(2,1)S(1)} %get-tuple-element.6, bf16[2,64,320]{1,2,0:T(8,128)(2,1)S(1)} %get-tuple-element.5), kind=kOutput, calls=%fused_computation.3 | convolution fusion | flops 339800064 | bytes 6553600 | tf_op jit(solution)/shard_map/rjgd,jdp->jrgp/dot_general | solution.py:58
  70.9 18.8 %pmax.7 = f32[2,256,8]{1,2,0:T(8,128)S(1)} all-reduce(f32[2,256,8]{1,2,0:T(8,128)S(1)} %get-tuple-element.9), channel_id=1, replica_groups=mesh['groups'=2,'tok'=4,'head'=4] {'tok'}, use_global_device_ids=true, to_apply=%region_4.5 | all-reduce | flops 4096 | bytes 32768 | tf_op jit(solution)/shard_map/pmax | solution.py:63
  89.6 3.9 %fusion.8 = f32[2,128,256,8]{2,1,3,0:T(8,128)S(1)} fusion(bf16[2,1,128,320]{2,1,0,3:T(2,128)(2,1)S(1)} %slice.17, f32[2,320,256,8]{2,1,3,0:T(8,128)} %get-tuple-element.10, f32[2,256,8]{1,2,0:T(8,128)S(1)} %pmax.7, pred[256,320]{0,1:T(8,128)(4,1)S(1)} %broadcast_compare_fusion), kind=kOutput, calls=%fused_computation.21 | convolution fusion | flops 340787200 | bytes 7602176 | tf_op jit(solution)/shard_map/jrgp,jdp->rjgd/dot_general | solution.py:65
  93.5 1.9 %copy.23 = f32[256,2048]{1,0:T(8,128)} copy(f32[256,2048]{0,1:T(8,128)S(1)} %bitcast.63) | data formatting | bytes 4194304 | tf_op jit(solution)/shard_map/reshape | solution.py:66
  95.4 0.0 all-reduce.3.cloned.1.call-update
  95.4 3.6 %convert_reduce_fusion = f32[2,256,8]{1,2,0:T(8,128)S(1)} fusion(f32[2,256,8]{1,2,0:T(8,128)S(1)} %pmax.7, f32[2,320,256,8]{2,1,3,0:T(8,128)} %get-tuple-element.10, pred[256,320]{0,1:T(8,128)(4,1)S(1)} %broadcast_compare_fusion), kind=kLoop, calls=%fused_computation.1 | loop fusion | flops 7860224 | bytes 5357568 | tf_op jit(solution)/shard_map/reduce_sum | solution.py:68
  99.0 16.7 %psum.23 = f32[256,16]{0,1:T(8,128)S(1)} all-reduce(f32[256,16]{0,1:T(8,128)S(1)} %bitcast.69), channel_id=1, replica_groups=mesh['groups'=2,'tok'=4,'head'=4] {'tok'}, use_global_device_ids=true, to_apply=%region_7.8 | all-reduce | flops 4096 | bytes 32768 | tf_op jit(solution)/shard_map/psum | solution.py:73
  115.7 0.1 constant_dynamic-slice_fusion
  115.8 0.1 copy.24
  115.9 63.5 %all-reduce.3.cloned.1.call-done = f32[256,2048]{1,0:T(8,128)} async-done(((f32[256,2048]{1,0:T(8,128)}), f32[256,2048]{1,0:T(8,128)}) %all-reduce.3.cloned.1.call-update) | async-done | bytes 2097168 | tf_op jit(solution)/shard_map/psum | solution.py:73
  179.3 0.2 div.27
  179.5 2.0 %fusion.4 = bf16[64,2048]{1,0:T(8,128)(2,1)} fusion(f32[8,8,16,128]{3,2,1,0:T(8,128)S(1)} %bitcast.68, f32[256,2048]{1,0:T(8,128)} %all-reduce.3.cloned.1.call-done, s32[]{:T(128)S(6)} %select_n.9), kind=kLoop, calls=%fused_computation.13 | loop fusion | flops 262144 | bytes 1310724 | tf_op jit(solution)/shard_map/convert_element_type | solution.py:78
  (6 shorter events, 0.0 us)
Async XLA Ops:
  7.4 34.7 %all-gather.2.cloned.1.call-start = ((), (), s32[]{:S(2)}) async-start(), calls=%async_computation.2 | async-start | bytes 1310720 | tf_op jit(solution)/shard_map/all_gather | solution.py:38
  8.1 57.2 %reduce-scatter.2.cloned.1.call-start = ((), (), s32[]{:S(2)}) async-start(), calls=%async_computation.1 | async-start | bytes 3276800 | tf_op jit(solution)/shard_map/reduce_scatter | solution.py:45
  18.2 4.8 %copy-start = (bf16[320,2048]{1,0:T(8,128)(2,1)S(1)}, bf16[320,2048]{1,0:T(8,128)(2,1)}, u32[]{:S(2)}) copy-start(bf16[320,2048]{1,0:T(8,128)(2,1)} %param.7) | copy-start | bytes 3932164
  18.2 4.8 %copy-start.2 = (bf16[2048,1024]{1,0:T(8,128)(2,1)S(1)}, bf16[2048,1024]{1,0:T(8,128)(2,1)}, u32[]{:S(2)}) copy-start(bf16[2048,1024]{1,0:T(8,128)(2,1)} %param.10) | copy-start | bytes 12582916
  18.2 4.8 %copy-start.3 = (f32[2048]{0:T(1024)S(1)}, f32[2048]{0:T(1024)}, u32[]{:S(2)}) copy-start(f32[2048]{0:T(1024)} %param.9) | copy-start | bytes 24580
  30.4 0.7 copy-start.1
  30.4 0.7 copy-start.5
  30.4 1.9 %copy-start.4 = (s32[64]{0:T(128)S(1)}, s32[64]{0:T(128)}, u32[]{:S(2)}) copy-start(s32[64]{0:T(128)} %param.13) | copy-start | bytes 772
  30.5 148.9 %all-reduce.3.cloned.1.call-start = ((), (), s32[]{:S(2)}) async-start(), calls=%async_computation.3 | async-start | bytes 4194304 | tf_op jit(solution)/shard_map/psum | solution.py:73
Sparse Core Ops, SparseCore 0:
  9.7 30.7 all-gather.1
  95.6 83.7 all-reduce.2
Sparse Core Ops, SparseCore 1:
  30.6 34.6 reduce-scatter.1
where the time goes:
time: 189 us
  waiting for transfers between devices  85.9 us (45%)
  blocking collectives  52.5 us (28%)
  between operations  15.7 us (8%)
  matrix products  13.3 us (7%)
  local copies, waits for them, and re-layouts  11 us (6%)
  other arithmetic  10.5 us (6%)
    psum x1, waiting for transfers between devices, body(): numer_all, denom_all = lax.psum((numer, denom), 'tok')  63.5 us
    reduce_scatter x1, waiting for transfers between devices, body(): lax.psum_scatter(jnp.stack((key_term, value_term), axis=1).reshape(heads...  21.7 us
    pmax x1, blocking collectives, body(): top = lax.pmax(jnp.max(scores, axis=3), 'tok')  18.8 us
    psum x1, blocking collectives, body(): numer_all, denom_all = lax.psum((numer, denom), 'tok')  16.7 us
    unnamed x1, blocking collectives  8.63 us
    psum x1, blocking collectives, body(): squares = lax.psum(jnp.sum(wide * wide, axis=1), 'head')  8.36 us
    dot_general x2, matrix products, project_columns(): lax.dot_general(weight_rows, normed_piece, (((0,), (1,)), ((), ())), pref...  6.07 us
    dot_general x1, matrix products, body(): jnp.einsum('jrgp,jdp->rjgd', weights, values_t, preferred_element_type=jn...  3.87 us
  transfers between devices with their start and end apart: 3, of which 2 were waited for; matrix products, arithmetic and copies ran while one was open for 11% of the time, Pallas kernels for 0%

commit v1 on v0

v1 whole, which is shorter than its diff:
```python
import functools

import jax
import jax.numpy as jnp
from jax import lax
from jax.experimental import pallas as pl
from jax.experimental.pallas import tpu as pltpu
from jax.sharding import PartitionSpec as P

HD = 128
QPK = 8
THETA = 500000.0
EPS = 1e-05
W_PARTS = 4
TOK_SPLIT = 2
WIRE = jnp.bfloat16
MESH = pl.DeviceIdType.MESH


def kernel(
    T, H, full_width,
    hidden_hbm, pos_ref, gain_ref, wk_hbm, wv_hbm, q_hbm, len_ref,
    out_ref,
    hid, normed, wbuf, qbuf, squares, cos_buf, sin_buf, pos_all, mask_len,
    pair_send, pair_recv, keep, x_send, x_recv, kv, scores, top_lanes, numer, denom,
    load_sem, sq_send, sq_recv, pos_send, pos_recv,
    pair_ssem, pair_rsem, x_ssem, x_rsem, z_ssem, z_rsem,
):
    X = H // 2
    n_tok, width = hid.shape
    kw = kv.shape[-1]
    kv_here = kw // HD
    rows = qbuf.shape[0]
    nt = n_tok // TOK_SPLIT
    t = lax.axis_index("tok")
    head = lax.axis_index("head")
    xi, core = head // 2, lax.rem(head, 2)
    partner = xi * 2 + (1 - core)

    loads = [pltpu.make_async_copy(hidden_hbm, hid, load_sem.at[0])]
    w_loads = []
    part = width // W_PARTS
    for which, src in enumerate((wk_hbm, wv_hbm)):
        group = []
        for i in range(W_PARTS):
            group.append(
                pltpu.make_async_copy(
                    src.at[pl.ds(i * part, part)],
                    wbuf.at[which, pl.ds(i * part, part)],
                    load_sem.at[2 + which * W_PARTS + i],
                )
            )
        w_loads.append(group)
    q_load = pltpu.make_async_copy(q_hbm, qbuf, load_sem.at[1])
    loads[0].start()
    for group in w_loads:
        for c in group:
            c.start()
    q_load.start()

    barrier = pltpu.get_barrier_semaphore()
    for d in range(1, H):
        pl.semaphore_signal(
            barrier, inc=1, device_id={"head": lax.rem(head + d, H)}, device_id_type=MESH
        )
    for d in range(1, T):
        pl.semaphore_signal(
            barrier, inc=1, device_id={"tok": lax.rem(t + d, T)}, device_id_type=MESH
        )

    loads[0].wait()
    acc = jnp.zeros((n_tok, HD), jnp.float32)
    for i in range(width // HD):
        piece = hid[:, i * HD:(i + 1) * HD].astype(jnp.float32)
        acc = acc + piece * piece
    local = jnp.sum(acc.T, axis=0, keepdims=True)
    squares[pl.ds(head, 1)] = jnp.broadcast_to(local, (8, n_tok))[None]

    pl.semaphore_wait(barrier, H - 1 + T - 1)
    sq_copies = []
    for d in range(1, H):
        c = pltpu.make_async_remote_copy(
            src_ref=squares.at[head], dst_ref=squares.at[head],
            send_sem=sq_send.at[d], recv_sem=sq_recv.at[d],
            device_id={"head": lax.rem(head + d, H)}, device_id_type=MESH,
        )
        c.start()
        sq_copies.append(c)
    pos_copies = []
    for d in range(1, T):
        c = pltpu.make_async_remote_copy(
            src_ref=pos_ref, dst_ref=pos_all.at[t],
            send_sem=pos_send.at[d], recv_sem=pos_recv.at[d],
            device_id={"tok": lax.rem(t + d, T)}, device_id_type=MESH,
        )
        c.start()
        pos_copies.append(c)
    pos_all[pl.ds(t, 1)] = pos_ref[...][None]

    pos_col = jnp.broadcast_to(pos_ref[...].astype(jnp.float32), (HD, n_tok)).T
    lane = lax.broadcasted_iota(jnp.int32, (1, HD), 1)
    half = HD // 2
    idx = jnp.where(lane < half, lane, lane - half).astype(jnp.float32)
    freq = THETA ** (-(idx * 2.0) / HD)
    angle = pos_col * freq
    cos_buf[...] = jnp.cos(angle)
    sine = jnp.sin(angle)
    sin_buf[...] = jnp.where(lane < half, -sine, sine)
    mask_len[...] = jnp.broadcast_to(len_ref[...].astype(jnp.float32), (HD, rows)).T.astype(jnp.int32)

    for c in sq_copies:
        c.wait()
    total = squares[0]
    for i in range(1, H):
        total = total + squares[i]
    r = lax.rsqrt(total[0:1] / full_width + EPS)
    r_col = jnp.broadcast_to(r, (HD, n_tok)).T
    for i in range(width // HD):
        cols = slice(i * HD, (i + 1) * HD)
        wide = hid[:, cols].astype(jnp.float32)
        normed[:, cols] = (wide * r_col * gain_ref[:, cols]).astype(jnp.bfloat16)

    units = [(which, th) for which in range(2) for th in range(TOK_SPLIT)]

    def project(which, th, block):
        cols = pl.ds(pl.multiple_of(block * kw, kw), kw)
        return jnp.dot(
            normed[th * nt:(th + 1) * nt, :], wbuf[which, :, cols],
            preferred_element_type=jnp.float32,
        )

    def pair_copy(u, dx):
        return pltpu.make_async_remote_copy(
            src_ref=pair_send.at[u, dx], dst_ref=pair_recv.at[u, dx],
            send_sem=pair_ssem.at[u, dx], recv_sem=pair_rsem.at[u, dx],
            device_id={"head": partner}, device_id_type=MESH,
        )

    def x_copy(u, dx):
        return pltpu.make_async_remote_copy(
            src_ref=x_send.at[u, dx - 1], dst_ref=x_recv.at[u, dx - 1],
            send_sem=x_ssem.at[u, dx - 1], recv_sem=x_rsem.at[u, dx - 1],
            device_id={"head": lax.rem(xi + dx, X) * 2 + core}, device_id_type=MESH,
        )

    def kv_at(u, block):
        which, th = units[u]
        return kv.at[block, which, pl.ds(th * nt, nt)]

    def z_copy(u, direction, step, block):
        to = lax.rem(t + 1, T) if direction == 0 else lax.rem(t + T - 1, T)
        return pltpu.make_async_remote_copy(
            src_ref=kv_at(u, block), dst_ref=kv_at(u, block),
            send_sem=z_ssem.at[direction, step, u], recv_sem=z_rsem.at[direction, step, u],
            device_id={"tok": to}, device_id_type=MESH,
        )

    def can_send(direction, step):
        if direction == 0:
            return jnp.logical_and(t + 1 < T, t - step >= 0)
        return jnp.logical_and(t - 1 >= 0, t + step < T)

    def can_recv(direction, step):
        if direction == 0:
            return t - 1 - step >= 0
        return t + 1 + step < T

    def arriving(direction, step):
        block = t - 1 - step if direction == 0 else t + 1 + step
        return jnp.clip(block, 0, T - 1)

    def leaving(direction, step):
        block = t - step if direction == 0 else t + step
        return jnp.clip(block, 0, T - 1)

    def stage_matmul(u):
        which, th = units[u]
        for dx in list(range(1, X)) + [0]:
            to = lax.rem(xi + dx, X)
            pair_send[u, dx] = project(which, th, to * 2 + (1 - core))
            pair_copy(u, dx).start()
            keep[u, dx] = project(which, th, to * 2 + core)

    def stage_chip(u):
        for dx in range(1, X):
            pair_copy(u, dx).wait_recv()
            x_send[u, dx - 1] = (keep[u, dx] + pair_recv[u, dx]).astype(WIRE)
            x_copy(u, dx).start()

    def stage_finish(u):
        which, th = units[u]
        pair_copy(u, 0).wait_recv()
        whole = keep[u, 0] + pair_recv[u, 0]
        for dx in range(1, X):
            x_copy(u, dx).wait_recv()
            whole = whole + x_recv[u, dx - 1].astype(jnp.float32)
        if which == 0:
            cosine = cos_buf[th * nt:(th + 1) * nt]
            sine = sin_buf[th * nt:(th + 1) * nt]
            pieces = []
            for j in range(kv_here):
                k = whole[:, j * HD:(j + 1) * HD]
                pieces.append(k * cosine + pltpu.roll(k, half, 1) * sine)
            whole = jnp.concatenate(pieces, axis=1) if kv_here > 1 else pieces[0]
        kv[pl.ds(t, 1), which, th * nt:(th + 1) * nt] = whole.astype(jnp.bfloat16)[None]
        for direction in range(2):
            @pl.when(can_send(direction, 0))
            def _():
                z_copy(u, direction, 0, t).start()

    n_units = len(units)
    for u in range(n_units):
        which, th = units[u]
        if th == 0:
            for c in w_loads[which]:
                c.wait()
        stage_matmul(u)
        stage_chip(u)
        if u > 0:
            stage_finish(u - 1)
    stage_finish(n_units - 1)

    q_load.wait()
    for c in pos_copies:
        c.wait()

    top_lanes[...] = jnp.full(top_lanes.shape, -1e30, jnp.float32)
    scale = HD ** (-0.5)

    def score_block(block):
        valid = pos_all[block] < mask_len[:, :1]
        for j in range(kv_here):
            k = kv[block, 0, :, j * HD:(j + 1) * HD]
            for g in range(QPK):
                q = qbuf[:, (j * QPK + g) * HD:(j * QPK + g + 1) * HD]
                s = lax.dot_general(
                    q, k, (((1,), (1,)), ((), ())), preferred_element_type=jnp.float32
                ) * scale
                s = jnp.where(valid, s, -1e30)
                scores[block, j * QPK + g] = s
                top_lanes[j * QPK + g] = jnp.maximum(
                    top_lanes[j * QPK + g], jnp.max(s, axis=1, keepdims=True)
                )

    def value_block(block):
        for j in range(kv_here):
            v = kv[block, 1, :, j * HD:(j + 1) * HD]
            for g in range(QPK):
                e = j * QPK + g
                w = jnp.exp(scores[block, e] - top_lanes[e][:, :1]).astype(jnp.bfloat16)
                denom[e] += jnp.sum(w.astype(jnp.float32), axis=1, keepdims=True)
                numer[e] += jnp.dot(w, v, preferred_element_type=jnp.float32)

    numer[...] = jnp.zeros(numer.shape, jnp.float32)
    denom[...] = jnp.zeros(denom.shape, jnp.float32)
    score_block(t)
    k_units = [u for u in range(n_units) if units[u][0] == 0]
    v_units = [u for u in range(n_units) if units[u][0] == 1]

    def arrive(us, direction, step):
        for u in us:
            z_copy(u, direction, step, arriving(direction, step)).wait_recv()
            if step + 1 < T - 1:
                @pl.when(can_send(direction, step + 1))
                def _():
                    z_copy(u, direction, step + 1, leaving(direction, step + 1)).start()

    for step in range(T - 1):
        for us in (k_units, v_units):
            if us is v_units and step == T - 2:
                continue
            for direction in range(2):
                @pl.when(can_recv(direction, step))
                def _():
                    arrive(us, direction, step)
                    if us is k_units:
                        score_block(arriving(direction, step))
    value_block(t)
    for step in range(T - 1):
        for direction in range(2):
            @pl.when(can_recv(direction, step))
            def _():
                if step == T - 2:
                    arrive(v_units, direction, step)
                value_block(arriving(direction, step))
    for e in range(kv_here * QPK):
        out_ref[:, e * HD:(e + 1) * HD] = (numer[e] / denom[e]).astype(jnp.bfloat16)

    for u in range(n_units):
        for dx in range(X):
            pair_copy(u, dx).wait_send()
        for dx in range(1, X):
            x_copy(u, dx).wait_send()
        for step in range(T - 1):
            for direction in range(2):
                @pl.when(can_send(direction, step))
                def _():
                    z_copy(u, direction, step, leaving(direction, step)).wait_send()


def body(hidden, positions, norm_gain, w_key, w_value, queries, lengths):
    T, H = lax.axis_size("tok"), lax.axis_size("head")
    X = H // 2
    n_tok, width = hidden.shape
    rows, q_cols = queries.shape
    kw = w_key.shape[1] // H
    e = q_cols // HD
    nt = n_tok // TOK_SPLIT
    n_units = 2 * TOK_SPLIT
    f32, bf16 = jnp.float32, jnp.bfloat16
    vmem = pl.BlockSpec(memory_space=pltpu.VMEM)
    hbm = pl.BlockSpec(memory_space=pl.ANY)
    dma = pltpu.SemaphoreType.DMA
    scratch = [
        pltpu.VMEM((n_tok, width), bf16),
        pltpu.VMEM((n_tok, width), bf16),
        pltpu.VMEM((2, width, w_key.shape[1]), bf16),
        pltpu.VMEM((rows, q_cols), bf16),
        pltpu.VMEM((H, 8, n_tok), f32),
        pltpu.VMEM((n_tok, HD), f32),
        pltpu.VMEM((n_tok, HD), f32),
        pltpu.VMEM((T, 1, n_tok), jnp.int32),
        pltpu.VMEM((rows, HD), jnp.int32),
        pltpu.VMEM((n_units, X, nt, kw), f32),
        pltpu.VMEM((n_units, X, nt, kw), f32),
        pltpu.VMEM((n_units, X, nt, kw), f32),
        pltpu.VMEM((n_units, X - 1, nt, kw), WIRE),
        pltpu.VMEM((n_units, X - 1, nt, kw), WIRE),
        pltpu.VMEM((T, 2, n_tok, kw), bf16),
        pltpu.VMEM((T, e, rows, n_tok), f32),
        pltpu.VMEM((e, rows, HD), f32),
        pltpu.VMEM((e, rows, HD), f32),
        pltpu.VMEM((e, rows, HD), f32),
        dma((2 + 2 * W_PARTS,)),
        dma((H,)), dma((H,)),
        dma((T,)), dma((T,)),
        dma((n_units, X)), dma((n_units, X)),
        dma((n_units, X - 1)), dma((n_units, X - 1)),
        dma((2, T - 1, n_units)), dma((2, T - 1, n_units)),
    ]
    return pl.pallas_call(
        functools.partial(kernel, T, H, width * H),
        out_shape=jax.ShapeDtypeStruct((rows, q_cols), bf16),
        in_specs=[hbm, vmem, vmem, hbm, hbm, hbm, vmem],
        out_specs=vmem,
        scratch_shapes=scratch,
        compiler_params=pltpu.CompilerParams(
            collective_id=0, has_side_effects=True, vmem_limit_bytes=60 * 1024 * 1024
        ),
    )(
        hidden, positions.reshape(1, n_tok), norm_gain.reshape(1, width), w_key, w_value,
        queries, lengths.reshape(1, rows),
    )


def solution(mesh):
    in_specs = (
        P(("groups", "tok"), "head"),
        P(("groups", "tok")),
        P("head"),
        P("head", None),
        P("head", None),
        P(("groups", "tok"), "head"),
        P(("groups", "tok")),
    )
    out_specs = P(("groups", "tok"), "head")
    return jax.shard_map(body, mesh=mesh, in_specs=in_specs, out_specs=out_specs, check_vma=False)
```

time: 189 us -> 47.8 us (0.25)
  waiting for transfers between devices: 85.9 us -> 0 us
  blocking collectives: 52.5 us -> 0 us
  Pallas kernels: 0 us -> 44.7 us
  between operations: 15.7 us -> 0.01 us
  matrix products: 13.3 us -> 0 us
  other arithmetic: 10.5 us -> 0 us
  local copies, waits for them, and re-layouts: 11 us -> 2.91 us
    psum x1 -> x0, waiting for transfers between devices: 63.5 us -> none  [body(): numer_all, denom_all = lax.psum((numer, denom), 'tok')]
    pallas_call x0 -> x1, Pallas kernels: none -> 44.7 us  [body(): pl.pallas_call(functools.partial(kernel, T, H, width * H), out_shape=jax....]
    psum x2 -> x0, blocking collectives: 25.1 us -> none  [the longest x1 16.7 us: body(): numer_all, denom_all = lax.psum((numer, denom), 'tok')]
    reduce_scatter x1 -> x0, waiting for transfers between devices: 21.7 us -> none  [body(): lax.psum_scatter(jnp.stack((key_term, value_term), axis=1).reshape(heads...]
    pmax x1 -> x0, blocking collectives: 18.8 us -> none  [body(): top = lax.pmax(jnp.max(scores, axis=3), 'tok')]
    dot_general x4 -> x0, matrix products: 13.3 us -> none  [the longest x2 6.07 us: project_columns(): lax.dot_general(weight_rows, normed_piece, (((0,), (1,)), ((), ())), pref...]
    unnamed x1 -> x0, blocking collectives: 8.63 us -> none
    reshape x3 -> x1, local copies, waits for them, and re-layouts: 6.62 us -> 1.24 us  [body(): positions.reshape(1, n_tok)]
  transfers between devices with their start and end apart: 3 -> 0, of which waited for: 2 -> 0; matrix products, arithmetic and copies ran while one was open for 11% -> 0% of each run, Pallas kernels for 0% -> 0%
where the time goes in v1:
time: 47.8 us; the launch traced here: 47.6 us
  Pallas kernels  44.7 us (94%)
  local copies, waits for them, and re-layouts  2.91 us (6%)
    pallas_call x1, Pallas kernels, body(): pl.pallas_call(functools.partial(kernel, T, H, width * H), out_shape=jax....  44.7 us
    unnamed x1, local copies, waits for them, and re-layouts  1.67 us
    reshape x1, local copies, waits for them, and re-layouts, body(): positions.reshape(1, n_tok)  1.24 us

profile of v1, /device:TPU:0, one launch (start us, length us, event | category | flops | bytes accessed | tf_op | source)
XLA Modules:
  0.0 47.6 jit_solution(149792266407957196)
XLA Ops:
  0.0 1.2 %reshape.9.pos_ref = s32[1,320]{1,0:T(1,128)} reshape(s32[320]{0:T(512)} %param.8) | data formatting | bytes 2560 | tf_op jit(solution)/shard_map/reshape | solution.py:351
  1.2 44.7 %shard_map.73 = bf16[64,2048]{1,0:T(8,128)(2,1)} custom-call(bf16[320,2048]{1,0:T(8,128)(2,1)} %hidden_hbm.1, s32[1,320]{1,0:T(1,128)} %reshape.9.pos_ref, f32[1,2048]{1,0:T(1,128)} %bitcast.2, bf16[2048,1024]{1,0:T(8,128)(2,1)} %wk_hbm.1, bf16[2048,1024]{1,0:T(8,128)(2,1)} %wv_hbm.1, bf16[64,2048]{1,0:T(8,128)(2,1)} %q_hbm.1, s32[1,64]{1,0:T(1,128)} %bitcast.3), custom_call_target="tpu_custom_call" | custom-call | tf_op jit(solution)/shard_map/pallas_call | solution.py:341
  46.0 1.7 %copy.9 = bf16[64,2048]{1,0:T(8,128)(2,1)} copy(bf16[64,2048]{1,0:T(8,128)(2,1)} %shard_map.73) | data formatting | bytes 524288

commit v2 on v1

v2 whole, which is shorter than its diff:
```python
import functools

import jax
import jax.numpy as jnp
from jax import lax
from jax.experimental import pallas as pl
from jax.experimental.pallas import tpu as pltpu
from jax.sharding import PartitionSpec as P

HD = 128
QPK = 8
THETA = 500000.0
EPS = 1e-05
H_PARTS = 4
TOK_SPLIT = 2
WIRE = jnp.bfloat16
MESH = pl.DeviceIdType.MESH


def kernel(
    T, H, full_width,
    hidden_hbm, pos_ref, gain_ref, wk_hbm, wv_hbm, q_hbm, len_ref,
    out_ref,
    hid, normed, wbuf, qbuf, squares, cos_buf, sin_buf, pos_all, mask_len,
    pair_send, pair_recv, keep, x_send, x_recv, kv, scores, top_lanes, numer, denom,
    load_sem, sq_send, sq_recv, pos_send, pos_recv,
    pair_ssem, pair_rsem, x_ssem, x_rsem, z_ssem, z_rsem,
    q_extra, len_extra, mask_extra, far_out, far_stats, near_out, near_stats, off_ssem, off_rsem,
):
    X = H // 2
    n_tok, width = hid.shape
    kw = kv.shape[-1]
    kv_here = kv.shape[1]
    rows = qbuf.shape[0]
    nt = n_tok // TOK_SPLIT
    t = lax.axis_index("tok")
    head = lax.axis_index("head")
    xi, core = head // 2, lax.rem(head, 2)
    partner = xi * 2 + (1 - core)
    order = list(reversed(range(kv_here)))
    offload = kv_here > 1 and T >= 4
    moved = kv_here - 1 if offload else -1
    is_client = jnp.logical_or(t == 0, t == T - 1)
    is_helper = jnp.logical_or(t == 1, t == T - 2)
    other_end = jnp.where(t < T // 2, jnp.where(t == 0, 1, 0), jnp.where(t == T - 1, T - 2, T - 1))

    part = n_tok // H_PARTS
    h_loads = [
        pltpu.make_async_copy(
            hidden_hbm.at[pl.ds(i * part, part)], hid.at[pl.ds(i * part, part)], load_sem.at[1 + i]
        )
        for i in range(H_PARTS)
    ]
    w_loads = []
    at = 1 + H_PARTS
    for j in order:
        group = []
        for blk in range(H):
            for which, src in enumerate((wk_hbm, wv_hbm)):
                h = blk * kv_here + j
                group.append(
                    pltpu.make_async_copy(
                        src.at[:, pl.ds(h * HD, HD)],
                        wbuf.at[:, pl.ds(h * kw + which * HD, HD)],
                        load_sem.at[at],
                    )
                )
                at += 1
        w_loads.append(group)
    q_load = pltpu.make_async_copy(q_hbm, qbuf, load_sem.at[0])
    for c in h_loads:
        c.start()
    q_load.start()

    barrier = pltpu.get_barrier_semaphore()
    for d in range(1, H):
        pl.semaphore_signal(
            barrier, inc=1, device_id={"head": lax.rem(head + d, H)}, device_id_type=MESH
        )
    for d in range(1, T):
        pl.semaphore_signal(
            barrier, inc=1, device_id={"tok": lax.rem(t + d, T)}, device_id_type=MESH
        )

    sums = []
    for p in range(H_PARTS):
        h_loads[p].wait()
        acc = jnp.zeros((part, HD), jnp.float32)
        for i in range(width // HD):
            piece = hid[p * part:(p + 1) * part, i * HD:(i + 1) * HD].astype(jnp.float32)
            acc = acc + piece * piece
        sums.append(acc)
    for group in w_loads:
        for c in group:
            c.start()
    acc = jnp.concatenate(sums, axis=0)
    local = jnp.sum(acc.T, axis=0, keepdims=True)
    squares[pl.ds(head, 1)] = jnp.broadcast_to(local, (8, n_tok))[None]

    pl.semaphore_wait(barrier, H - 1 + T - 1)
    sq_copies = []
    for d in range(1, H):
        c = pltpu.make_async_remote_copy(
            src_ref=squares.at[head], dst_ref=squares.at[head],
            send_sem=sq_send.at[d], recv_sem=sq_recv.at[d],
            device_id={"head": lax.rem(head + d, H)}, device_id_type=MESH,
        )
        c.start()
        sq_copies.append(c)
    pos_copies = []
    for d in range(1, T):
        c = pltpu.make_async_remote_copy(
            src_ref=pos_ref, dst_ref=pos_all.at[t],
            send_sem=pos_send.at[d], recv_sem=pos_recv.at[d],
            device_id={"tok": lax.rem(t + d, T)}, device_id_type=MESH,
        )
        c.start()
        pos_copies.append(c)
    pos_all[pl.ds(t, 1)] = pos_ref[...][None]

    def off_copy(i, src, dst):
        return pltpu.make_async_remote_copy(
            src_ref=src, dst_ref=dst, send_sem=off_ssem.at[i], recv_sem=off_rsem.at[i],
            device_id={"tok": other_end}, device_id_type=MESH,
        )

    def ask_copies():
        cols = pl.ds(moved * QPK * HD, QPK * HD)
        return off_copy(0, qbuf.at[:, cols], q_extra), off_copy(1, len_ref, len_extra)

    def answer_copies():
        return off_copy(2, far_out, near_out), off_copy(3, far_stats, near_stats)

    q_load.wait()
    if offload:
        @pl.when(is_client)
        def _():
            for c in ask_copies():
                c.start()

    pos_col = jnp.broadcast_to(pos_ref[...].astype(jnp.float32), (HD, n_tok)).T
    lane = lax.broadcasted_iota(jnp.int32, (1, HD), 1)
    half = HD // 2
    idx = jnp.where(lane < half, lane, lane - half).astype(jnp.float32)
    freq = THETA ** (-(idx * 2.0) / HD)
    angle = pos_col * freq
    cos_buf[...] = jnp.cos(angle)
    sine = jnp.sin(angle)
    sin_buf[...] = jnp.where(lane < half, -sine, sine)
    mask_len[...] = jnp.broadcast_to(len_ref[...].astype(jnp.float32), (HD, rows)).T.astype(jnp.int32)

    for c in sq_copies:
        c.wait()
    total = squares[0]
    for i in range(1, H):
        total = total + squares[i]
    r = lax.rsqrt(total[0:1] / full_width + EPS)
    r_col = jnp.broadcast_to(r, (HD, n_tok)).T
    for i in range(width // HD):
        cols = slice(i * HD, (i + 1) * HD)
        wide = hid[:, cols].astype(jnp.float32)
        normed[:, cols] = (wide * r_col * gain_ref[:, cols]).astype(jnp.bfloat16)

    units = [(j, th) for j in order for th in range(TOK_SPLIT)]

    def project(j, th, block):
        cols = pl.ds(pl.multiple_of((block * kv_here + j) * kw, kw), kw)
        return jnp.dot(
            normed[th * nt:(th + 1) * nt, :], wbuf[:, cols],
            preferred_element_type=jnp.float32,
        )

    def pair_copy(u, dx):
        return pltpu.make_async_remote_copy(
            src_ref=pair_send.at[u, dx], dst_ref=pair_recv.at[u, dx],
            send_sem=pair_ssem.at[u, dx], recv_sem=pair_rsem.at[u, dx],
            device_id={"head": partner}, device_id_type=MESH,
        )

    def x_copy(u, dx):
        return pltpu.make_async_remote_copy(
            src_ref=x_send.at[u, dx - 1], dst_ref=x_recv.at[u, dx - 1],
            send_sem=x_ssem.at[u, dx - 1], recv_sem=x_rsem.at[u, dx - 1],
            device_id={"head": lax.rem(xi + dx, X) * 2 + core}, device_id_type=MESH,
        )

    def kv_at(u, block):
        j, th = units[u]
        return kv.at[block, j, pl.ds(th * nt, nt)]

    def z_copy(u, direction, step, block):
        to = lax.rem(t + 1, T) if direction == 0 else lax.rem(t + T - 1, T)
        return pltpu.make_async_remote_copy(
            src_ref=kv_at(u, block), dst_ref=kv_at(u, block),
            send_sem=z_ssem.at[direction, step, u], recv_sem=z_rsem.at[direction, step, u],
            device_id={"tok": to}, device_id_type=MESH,
        )

    def can_send(direction, step, j):
        end = 1 if j == moved else 0
        if direction == 0:
            return jnp.logical_and(t + 1 < T - end, t - step >= 0)
        return jnp.logical_and(t - 1 >= end, t + step < T)

    def can_recv(direction, step, j):
        end = 1 if j == moved else 0
        if direction == 0:
            return jnp.logical_and(t < T - end, t - 1 - step >= 0)
        return jnp.logical_and(t >= end, t + 1 + step < T)

    def arriving(direction, step):
        block = t - 1 - step if direction == 0 else t + 1 + step
        return jnp.clip(block, 0, T - 1)

    def leaving(direction, step):
        block = t - step if direction == 0 else t + step
        return jnp.clip(block, 0, T - 1)

    def stage_matmul(u):
        j, th = units[u]
        for dx in list(range(1, X)) + [0]:
            to = lax.rem(xi + dx, X)
            pair_send[u, dx] = project(j, th, to * 2 + (1 - core))
            pair_copy(u, dx).start()
            keep[u, dx] = project(j, th, to * 2 + core)

    def stage_chip(u):
        for dx in range(1, X):
            pair_copy(u, dx).wait_recv()
            x_send[u, dx - 1] = (keep[u, dx] + pair_recv[u, dx]).astype(WIRE)
            x_copy(u, dx).start()

    def stage_finish(u):
        j, th = units[u]
        pair_copy(u, 0).wait_recv()
        whole = keep[u, 0] + pair_recv[u, 0]
        for dx in range(1, X):
            x_copy(u, dx).wait_recv()
            whole = whole + x_recv[u, dx - 1].astype(jnp.float32)
        cosine = cos_buf[th * nt:(th + 1) * nt]
        sine = sin_buf[th * nt:(th + 1) * nt]
        k = whole[:, :HD]
        k = k * cosine + pltpu.roll(k, half, 1) * sine
        rows_at = slice(th * nt, (th + 1) * nt)
        kv[pl.ds(t, 1), j, rows_at, :HD] = k.astype(jnp.bfloat16)[None]
        kv[pl.ds(t, 1), j, rows_at, HD:] = whole[:, HD:].astype(jnp.bfloat16)[None]
        for direction in range(2):
            @pl.when(can_send(direction, 0, j))
            def _():
                z_copy(u, direction, 0, t).start()

    n_units = len(units)
    for u in range(n_units):
        j, th = units[u]
        if th == 0:
            for c in w_loads[order.index(j)]:
                c.wait()
        stage_matmul(u)
        stage_chip(u)
        if u > 0:
            stage_finish(u - 1)
    stage_finish(n_units - 1)

    for c in pos_copies:
        c.wait()
    if offload:
        @pl.when(is_helper)
        def _():
            for c in ask_copies():
                c.wait_recv()
            mask_extra[...] = jnp.broadcast_to(
                len_extra[...].astype(jnp.float32), (HD, rows)
            ).T.astype(jnp.int32)

    heads = kv_here * QPK
    top_lanes[...] = jnp.full(top_lanes.shape, -1e30, jnp.float32)
    numer[...] = jnp.zeros(numer.shape, jnp.float32)
    denom[...] = jnp.zeros(denom.shape, jnp.float32)
    scale = HD ** (-0.5)

    def score_block(block, j, extra=False):
        k = kv[block, j, :, :HD]
        valid = pos_all[block] < (mask_extra if extra else mask_len)[:, :1]
        for g in range(QPK):
            e = heads + g if extra else j * QPK + g
            if extra:
                q = q_extra[:, g * HD:(g + 1) * HD]
            else:
                q = qbuf[:, e * HD:(e + 1) * HD]
            s = lax.dot_general(
                q, k, (((1,), (1,)), ((), ())), preferred_element_type=jnp.float32
            ) * scale
            s = jnp.where(valid, s, -1e30)
            scores[block, e] = s
            top_lanes[e] = jnp.maximum(top_lanes[e], jnp.max(s, axis=1, keepdims=True))

    def value_block(block, j, extra=False):
        v = kv[block, j, :, HD:]
        for g in range(QPK):
            e = heads + g if extra else j * QPK + g
            w = jnp.exp(scores[block, e] - top_lanes[e][:, :1]).astype(jnp.bfloat16)
            denom[e] += jnp.sum(w.astype(jnp.float32), axis=1, keepdims=True)
            numer[e] += jnp.dot(w, v, preferred_element_type=jnp.float32)

    def arrive(j, direction, step):
        for u in range(n_units):
            if units[u][0] != j:
                continue
            z_copy(u, direction, step, arriving(direction, step)).wait_recv()
            if step + 1 < T - 1:
                @pl.when(can_send(direction, step + 1, j))
                def _():
                    z_copy(u, direction, step + 1, leaving(direction, step + 1)).start()

    def values_of(j):
        value_block(t, j)
        for step in range(T - 1):
            for direction in range(2):
                @pl.when(can_recv(direction, step, j))
                def _():
                    value_block(arriving(direction, step), j)

    def serves(direction):
        return t == T - 2 if direction == 0 else t == 1

    def answer():
        value_block(t, moved, extra=True)
        for direction in range(2):
            @pl.when(serves(direction))
            def _():
                for step in range(T - 2):
                    value_block(arriving(direction, step), moved, extra=True)
        for g in range(QPK):
            e = heads + g
            far_out[g] = (numer[e] / denom[e]).astype(jnp.bfloat16)
            far_stats[0, g:g + 1] = top_lanes[e].T[0:1]
            far_stats[1, g:g + 1] = denom[e].T[0:1]
        for c in answer_copies():
            c.start()

    for j in order:
        score_block(t, j)
    if offload:
        @pl.when(is_helper)
        def _():
            score_block(t, moved, extra=True)
    for step in range(T - 1):
        for j in order:
            for direction in range(2):
                @pl.when(can_recv(direction, step, j))
                def _():
                    arrive(j, direction, step)
                    score_block(arriving(direction, step), j)
                if j == moved and step < T - 2:
                    @pl.when(serves(direction))
                    def _():
                        score_block(arriving(direction, step), j, extra=True)
            if j == moved and step == T - 3:
                @pl.when(is_helper)
                def _():
                    answer()
            if step == T - 2 and j != order[-1]:
                values_of(j)
    values_of(order[-1])
    for e in range(heads):
        if e // QPK != moved:
            out_ref[:, e * HD:(e + 1) * HD] = (numer[e] / denom[e]).astype(jnp.bfloat16)
    if offload:
        @pl.when(is_client)
        def _():
            for c in answer_copies():
                c.wait_recv()
            for g in range(QPK):
                e = moved * QPK + g
                far_top = jnp.broadcast_to(near_stats[0, g:g + 1], (HD, rows)).T
                far_den = jnp.broadcast_to(near_stats[1, g:g + 1], (HD, rows)).T
                top = jnp.maximum(top_lanes[e], far_top)
                a = jnp.exp(top_lanes[e] - top)
                b = jnp.exp(far_top - top) * far_den
                numer[e] = numer[e] * a + near_out[g].astype(jnp.float32) * b
                denom[e] = denom[e] * a + b
        for g in range(QPK):
            e = moved * QPK + g
            out_ref[:, e * HD:(e + 1) * HD] = (numer[e] / denom[e]).astype(jnp.bfloat16)

        @pl.when(is_client)
        def _():
            for c in ask_copies():
                c.wait_send()

        @pl.when(is_helper)
        def _():
            for c in answer_copies():
                c.wait_send()

    for u in range(n_units):
        for dx in range(X):
            pair_copy(u, dx).wait_send()
        for dx in range(1, X):
            x_copy(u, dx).wait_send()
        for step in range(T - 1):
            for direction in range(2):
                @pl.when(can_send(direction, step, units[u][0]))
                def _():
                    z_copy(u, direction, step, leaving(direction, step)).wait_send()


def body(hidden, positions, norm_gain, w_key, w_value, queries, lengths):
    T, H = lax.axis_size("tok"), lax.axis_size("head")
    X = H // 2
    n_tok, width = hidden.shape
    rows, q_cols = queries.shape
    kw = 2 * HD
    kv_here = w_key.shape[1] // HD // H
    e = q_cols // HD
    ex = e + QPK
    nt = n_tok // TOK_SPLIT
    n_units = kv_here * TOK_SPLIT
    f32, bf16 = jnp.float32, jnp.bfloat16
    vmem = pl.BlockSpec(memory_space=pltpu.VMEM)
    hbm = pl.BlockSpec(memory_space=pl.ANY)
    dma = pltpu.SemaphoreType.DMA
    scratch = [
        pltpu.VMEM((n_tok, width), bf16),
        pltpu.VMEM((n_tok, width), bf16),
        pltpu.VMEM((width, 2 * w_key.shape[1]), bf16),
        pltpu.VMEM((rows, q_cols), bf16),
        pltpu.VMEM((H, 8, n_tok), f32),
        pltpu.VMEM((n_tok, HD), f32),
        pltpu.VMEM((n_tok, HD), f32),
        pltpu.VMEM((T, 1, n_tok), jnp.int32),
        pltpu.VMEM((rows, HD), jnp.int32),
        pltpu.VMEM((n_units, X, nt, kw), f32),
        pltpu.VMEM((n_units, X, nt, kw), f32),
        pltpu.VMEM((n_units, X, nt, kw), f32),
        pltpu.VMEM((n_units, X - 1, nt, kw), WIRE),
        pltpu.VMEM((n_units, X - 1, nt, kw), WIRE),
        pltpu.VMEM((T, kv_here, n_tok, kw), bf16),
        pltpu.VMEM((T, ex, rows, n_tok), f32),
        pltpu.VMEM((ex, rows, HD), f32),
        pltpu.VMEM((ex, rows, HD), f32),
        pltpu.VMEM((ex, rows, HD), f32),
        dma((1 + H_PARTS + 2 * H * kv_here,)),
        dma((H,)), dma((H,)),
        dma((T,)), dma((T,)),
        dma((n_units, X)), dma((n_units, X)),
        dma((n_units, X - 1)), dma((n_units, X - 1)),
        dma((2, T - 1, n_units)), dma((2, T - 1, n_units)),
        pltpu.VMEM((rows, QPK * HD), bf16),
        pltpu.VMEM((1, rows), jnp.int32),
        pltpu.VMEM((rows, HD), jnp.int32),
        pltpu.VMEM((QPK, rows, HD), bf16),
        pltpu.VMEM((2, QPK, rows), f32),
        pltpu.VMEM((QPK, rows, HD), bf16),
        pltpu.VMEM((2, QPK, rows), f32),
        dma((4,)), dma((4,)),
    ]
    return pl.pallas_call(
        functools.partial(kernel, T, H, width * H),
        out_shape=jax.ShapeDtypeStruct((rows, q_cols), bf16),
        in_specs=[hbm, vmem, vmem, hbm, hbm, hbm, vmem],
        out_specs=vmem,
        scratch_shapes=scratch,
        compiler_params=pltpu.CompilerParams(
            collective_id=0, has_side_effects=True, vmem_limit_bytes=60 * 1024 * 1024
        ),
    )(
        hidden, positions.reshape(1, n_tok), norm_gain.reshape(1, width), w_key, w_value,
        queries, lengths.reshape(1, rows),
    )


def solution(mesh):
    in_specs = (
        P(("groups", "tok"), "head"),
        P(("groups", "tok")),
        P("head"),
        P("head", None),
        P("head", None),
        P(("groups", "tok"), "head"),
        P(("groups", "tok")),
    )
    out_specs = P(("groups", "tok"), "head")
    return jax.shard_map(body, mesh=mesh, in_specs=in_specs, out_specs=out_specs, check_vma=False)
```

time: 47.8 us -> 46.7 us (0.977)
  Pallas kernels: 44.7 us -> 43.6 us
    pallas_call x1, Pallas kernels: 44.7 us -> 43.6 us  [body(): pl.pallas_call(functools.partial(kernel, T, H, width * H), out_shape=jax....]
where the time goes in v2:
time: 46.7 us; the launch traced here: 46.5 us
  Pallas kernels  43.6 us (93%)
  local copies, waits for them, and re-layouts  2.91 us (6%)
    pallas_call x1, Pallas kernels, body(): pl.pallas_call(functools.partial(kernel, T, H, width * H), out_shape=jax....  43.6 us
    unnamed x1, local copies, waits for them, and re-layouts  1.67 us
    reshape x1, local copies, waits for them, and re-layouts, body(): positions.reshape(1, n_tok)  1.24 us

profile of v2, /device:TPU:0, one launch (start us, length us, event | category | flops | bytes accessed | tf_op | source)
XLA Modules:
  0.0 46.5 jit_solution(16848981616963630547)
XLA Ops:
  0.0 1.2 %reshape.9.pos_ref = s32[1,320]{1,0:T(1,128)} reshape(s32[320]{0:T(512)} %param.8) | data formatting | bytes 2560 | tf_op jit(solution)/shard_map/reshape | solution.py:468
  1.2 43.6 %shard_map.73 = bf16[64,2048]{1,0:T(8,128)(2,1)} custom-call(bf16[320,2048]{1,0:T(8,128)(2,1)} %hidden_hbm.1, s32[1,320]{1,0:T(1,128)} %reshape.9.pos_ref, f32[1,2048]{1,0:T(1,128)} %bitcast.2, bf16[2048,1024]{1,0:T(8,128)(2,1)} %wk_hbm.1, bf16[2048,1024]{1,0:T(8,128)(2,1)} %wv_hbm.1, bf16[64,2048]{1,0:T(8,128)(2,1)} %q_hbm.1, s32[1,64]{1,0:T(1,128)} %bitcast.3), custom_call_target="tpu_custom_call" | custom-call | tf_op jit(solution)/shard_map/pallas_call | solution.py:458
  44.8 1.7 %copy.9 = bf16[64,2048]{1,0:T(8,128)(2,1)} copy(bf16[64,2048]{1,0:T(8,128)(2,1)} %shard_map.73) | data formatting | bytes 524288

commit v3 on v2

--- a/solution.py
+++ b/solution.py
@@ -26,6 +26,7 @@
     load_sem, sq_send, sq_recv, pos_send, pos_recv,
     pair_ssem, pair_rsem, x_ssem, x_rsem, z_ssem, z_rsem,
     q_extra, len_extra, mask_extra, far_out, far_stats, near_out, near_stats, off_ssem, off_rsem,
+    q_stack,
 ):
     X = H // 2
     n_tok, width = hid.shape
@@ -82,6 +83,9 @@
             barrier, inc=1, device_id={"tok": lax.rem(t + d, T)}, device_id_type=MESH
         )
 
+    pos_row = pos_ref[...].reshape(1, n_tok)
+    pos_all[pl.ds(t, 1)] = pos_row[None]
+
     sums = []
     for p in range(H_PARTS):
         h_loads[p].wait()
@@ -95,7 +99,7 @@
             c.start()
     acc = jnp.concatenate(sums, axis=0)
     local = jnp.sum(acc.T, axis=0, keepdims=True)
-    squares[pl.ds(head, 1)] = jnp.broadcast_to(local, (8, n_tok))[None]
+    squares[pl.ds(head, 1)] = local[None]
 
     pl.semaphore_wait(barrier, H - 1 + T - 1)
     sq_copies = []
@@ -110,13 +114,12 @@
     pos_copies = []
     for d in range(1, T):
         c = pltpu.make_async_remote_copy(
-            src_ref=pos_ref, dst_ref=pos_all.at[t],
+            src_ref=pos_all.at[t], dst_ref=pos_all.at[t],
             send_sem=pos_send.at[d], recv_sem=pos_recv.at[d],
             device_id={"tok": lax.rem(t + d, T)}, device_id_type=MESH,
         )
         c.start()
         pos_copies.append(c)
-    pos_all[pl.ds(t, 1)] = pos_ref[...][None]
 
     def off_copy(i, src, dst):
         return pltpu.make_async_remote_copy(
@@ -138,7 +141,7 @@
             for c in ask_copies():
                 c.start()
 
-    pos_col = jnp.broadcast_to(pos_ref[...].astype(jnp.float32), (HD, n_tok)).T
+    pos_col = jnp.broadcast_to(pos_row.astype(jnp.float32), (HD, n_tok)).T
     lane = lax.broadcasted_iota(jnp.int32, (1, HD), 1)
     half = HD // 2
     idx = jnp.where(lane < half, lane, lane - half).astype(jnp.float32)
@@ -149,12 +152,15 @@
     sin_buf[...] = jnp.where(lane < half, -sine, sine)
     mask_len[...] = jnp.broadcast_to(len_ref[...].astype(jnp.float32), (HD, rows)).T.astype(jnp.int32)
 
+    for e in range(kv_here * QPK):
+        q_stack[e] = qbuf[:, e * HD:(e + 1) * HD]
+
     for c in sq_copies:
         c.wait()
     total = squares[0]
     for i in range(1, H):
         total = total + squares[i]
-    r = lax.rsqrt(total[0:1] / full_width + EPS)
+    r = lax.rsqrt(total / full_width + EPS)
     r_col = jnp.broadcast_to(r, (HD, n_tok)).T
     for i in range(width // HD):
         cols = slice(i * HD, (i + 1) * HD)
@@ -257,9 +263,8 @@
                 c.wait()
         stage_matmul(u)
         stage_chip(u)
-        if u > 0:
-            stage_finish(u - 1)
-    stage_finish(n_units - 1)
+    for u in range(n_units):
+        stage_finish(u)
 
     for c in pos_copies:
         c.wait()
@@ -271,6 +276,8 @@
             mask_extra[...] = jnp.broadcast_to(
                 len_extra[...].astype(jnp.float32), (HD, rows)
             ).T.astype(jnp.int32)
+            for g in range(QPK):
+                q_stack[kv_here * QPK + g] = q_extra[:, g * HD:(g + 1) * HD]
 
     heads = kv_here * QPK
     top_lanes[...] = jnp.full(top_lanes.shape, -1e30, jnp.float32)
@@ -278,29 +285,34 @@
     denom[...] = jnp.zeros(denom.shape, jnp.float32)
     scale = HD ** (-0.5)
 
+    group = QPK // 2
+
     def score_block(block, j, extra=False):
         k = kv[block, j, :, :HD]
-        valid = pos_all[block] < (mask_extra if extra else mask_len)[:, :1]
-        for g in range(QPK):
-            e = heads + g if extra else j * QPK + g
-            if extra:
-                q = q_extra[:, g * HD:(g + 1) * HD]
-            else:
-                q = qbuf[:, e * HD:(e + 1) * HD]
+        valid = (pos_all[block] < (mask_extra if extra else mask_len)[:, :1])[None]
+        slot = kv_here if extra else j
+        for half_at in range(0, QPK, group):
+            e = slice(slot * QPK + half_at, slot * QPK + half_at + group)
+            q = q_stack[e].reshape(group * rows, HD)
             s = lax.dot_general(
                 q, k, (((1,), (1,)), ((), ())), preferred_element_type=jnp.float32
-            ) * scale
+            ).reshape(group, rows, n_tok) * scale
             s = jnp.where(valid, s, -1e30)
             scores[block, e] = s
-            top_lanes[e] = jnp.maximum(top_lanes[e], jnp.max(s, axis=1, keepdims=True))
+            top_lanes[e] = jnp.maximum(top_lanes[e], jnp.max(s, axis=2, keepdims=True))
 
     def value_block(block, j, extra=False):
         v = kv[block, j, :, HD:]
-        for g in range(QPK):
-            e = heads + g if extra else j * QPK + g
-            w = jnp.exp(scores[block, e] - top_lanes[e][:, :1]).astype(jnp.bfloat16)
-            denom[e] += jnp.sum(w.astype(jnp.float32), axis=1, keepdims=True)
-            numer[e] += jnp.dot(w, v, preferred_element_type=jnp.float32)
+        v = jnp.concatenate([v, jnp.ones(v.shape, v.dtype)], axis=1)
+        slot = kv_here if extra else j
+        for half_at in range(0, QPK, group):
+            e = slice(slot * QPK + half_at, slot * QPK + half_at + group)
+            w = jnp.exp(scores[block, e] - top_lanes[e][:, :, :1]).astype(jnp.bfloat16)
+            both = jnp.dot(
+                w.reshape(group * rows, n_tok), v, preferred_element_type=jnp.float32
+            ).reshape(group, rows, 2 * HD)
+            numer[e] += both[:, :, :HD]
+            denom[e] += both[:, :, HD:]
 
     def arrive(j, direction, step):
         for u in range(n_units):
@@ -425,7 +437,7 @@
         pltpu.VMEM((n_tok, width), bf16),
         pltpu.VMEM((width, 2 * w_key.shape[1]), bf16),
         pltpu.VMEM((rows, q_cols), bf16),
-        pltpu.VMEM((H, 8, n_tok), f32),
+        pltpu.VMEM((H, 1, n_tok), f32),
         pltpu.VMEM((n_tok, HD), f32),
         pltpu.VMEM((n_tok, HD), f32),
         pltpu.VMEM((T, 1, n_tok), jnp.int32),
@@ -454,6 +466,7 @@
         pltpu.VMEM((QPK, rows, HD), bf16),
         pltpu.VMEM((2, QPK, rows), f32),
         dma((4,)), dma((4,)),
+        pltpu.VMEM((ex, rows, HD), bf16),
     ]
     return pl.pallas_call(
         functools.partial(kernel, T, H, width * H),
@@ -465,7 +478,7 @@
             collective_id=0, has_side_effects=True, vmem_limit_bytes=60 * 1024 * 1024
         ),
     )(
-        hidden, positions.reshape(1, n_tok), norm_gain.reshape(1, width), w_key, w_value,
+        hidden, positions, norm_gain.reshape(1, width), w_key, w_value,
         queries, lengths.reshape(1, rows),
     )
 

time: 46.7 us -> 43.1 us (0.923)
  Pallas kernels: 43.6 us -> 41.2 us
  local copies, waits for them, and re-layouts: 2.91 us -> 1.67 us
    pallas_call x1, Pallas kernels: 43.6 us -> 41.2 us  [body(): pl.pallas_call(functools.partial(kernel, T, H, width * H), out_shape=jax....]
    reshape x1 -> x0, local copies, waits for them, and re-layouts: 1.24 us -> none  [body(): positions.reshape(1, n_tok)]
where the time goes in v3:
time: 43.1 us; the launch traced here: 42.9 us
  Pallas kernels  41.2 us (96%)
  local copies, waits for them, and re-layouts  1.67 us (4%)
    pallas_call x1, Pallas kernels, body(): pl.pallas_call(functools.partial(kernel, T, H, width * H), out_shape=jax....  41.2 us
    unnamed x1, local copies, waits for them, and re-layouts  1.67 us

profile of v3, /device:TPU:0, one launch (start us, length us, event | category | flops | bytes accessed | tf_op | source)
XLA Modules:
  0.0 42.9 jit_solution(10415504787580709269)
XLA Ops:
  0.0 41.2 %shard_map.73 = bf16[64,2048]{1,0:T(8,128)(2,1)} custom-call(bf16[320,2048]{1,0:T(8,128)(2,1)} %hidden_hbm.1, s32[320]{0:T(512)} %pos_ref.1, f32[1,2048]{1,0:T(1,128)} %bitcast.2, bf16[2048,1024]{1,0:T(8,128)(2,1)} %wk_hbm.1, bf16[2048,1024]{1,0:T(8,128)(2,1)} %wv_hbm.1, bf16[64,2048]{1,0:T(8,128)(2,1)} %q_hbm.1, s32[1,64]{1,0:T(1,128)} %bitcast.3), custom_call_target="tpu_custom_call" | custom-call | tf_op jit(solution)/shard_map/pallas_call | solution.py:471
  41.2 1.7 %copy.9 = bf16[64,2048]{1,0:T(8,128)(2,1)} copy(bf16[64,2048]{1,0:T(8,128)(2,1)} %shard_map.73) | data formatting | bytes 524288

commit v4 on v3

--- a/solution.py
+++ b/solution.py
@@ -169,10 +169,10 @@
 
     units = [(j, th) for j in order for th in range(TOK_SPLIT)]
 
-    def project(j, th, block):
+    def project(j, block):
         cols = pl.ds(pl.multiple_of((block * kv_here + j) * kw, kw), kw)
         return jnp.dot(
-            normed[th * nt:(th + 1) * nt, :], wbuf[:, cols],
+            normed[...], wbuf[:, cols],
             preferred_element_type=jnp.float32,
         )
 
@@ -222,13 +222,17 @@
         block = t - step if direction == 0 else t + step
         return jnp.clip(block, 0, T - 1)
 
-    def stage_matmul(u):
-        j, th = units[u]
+    def stage_matmul(j):
+        mine = [(u, units[u][1]) for u in range(len(units)) if units[u][0] == j]
         for dx in list(range(1, X)) + [0]:
             to = lax.rem(xi + dx, X)
-            pair_send[u, dx] = project(j, th, to * 2 + (1 - core))
-            pair_copy(u, dx).start()
-            keep[u, dx] = project(j, th, to * 2 + core)
+            theirs = project(j, to * 2 + (1 - core))
+            for u, th in mine:
+                pair_send[u, dx] = theirs[th * nt:(th + 1) * nt]
+                pair_copy(u, dx).start()
+            ours = project(j, to * 2 + core)
+            for u, th in mine:
+                keep[u, dx] = ours[th * nt:(th + 1) * nt]
 
     def stage_chip(u):
         for dx in range(1, X):
@@ -256,13 +260,13 @@
                 z_copy(u, direction, 0, t).start()
 
     n_units = len(units)
-    for u in range(n_units):
-        j, th = units[u]
-        if th == 0:
-            for c in w_loads[order.index(j)]:
-                c.wait()
-        stage_matmul(u)
-        stage_chip(u)
+    for at, j in enumerate(order):
+        for c in w_loads[at]:
+            c.wait()
+        stage_matmul(j)
+        for u in range(n_units):
+            if units[u][0] == j:
+                stage_chip(u)
     for u in range(n_units):
         stage_finish(u)
 

time: 43.1 us -> 42.2 us (0.979)
  Pallas kernels: 41.2 us -> 40.3 us
    pallas_call x1, Pallas kernels: 41.2 us -> 40.3 us  [body(): pl.pallas_call(functools.partial(kernel, T, H, width * H), out_shape=jax....]
where the time goes in v4:
time: 42.2 us; the launch traced here: 42 us
  Pallas kernels  40.3 us (95%)
  local copies, waits for them, and re-layouts  1.67 us (4%)
    pallas_call x1, Pallas kernels, body(): pl.pallas_call(functools.partial(kernel, T, H, width * H), out_shape=jax....  40.3 us
    unnamed x1, local copies, waits for them, and re-layouts  1.67 us

profile of v4, /device:TPU:0, one launch (start us, length us, event | category | flops | bytes accessed | tf_op | source)
XLA Modules:
  0.0 42.0 jit_solution(89872895386127139)
XLA Ops:
  0.0 40.3 %shard_map.73 = bf16[64,2048]{1,0:T(8,128)(2,1)} custom-call(bf16[320,2048]{1,0:T(8,128)(2,1)} %hidden_hbm.1, s32[320]{0:T(512)} %pos_ref.1, f32[1,2048]{1,0:T(1,128)} %bitcast.2, bf16[2048,1024]{1,0:T(8,128)(2,1)} %wk_hbm.1, bf16[2048,1024]{1,0:T(8,128)(2,1)} %wv_hbm.1, bf16[64,2048]{1,0:T(8,128)(2,1)} %q_hbm.1, s32[1,64]{1,0:T(1,128)} %bitcast.3), custom_call_target="tpu_custom_call" | custom-call | tf_op jit(solution)/shard_map/pallas_call | solution.py:475
  40.3 1.7 %copy.9 = bf16[64,2048]{1,0:T(8,128)(2,1)} copy(bf16[64,2048]{1,0:T(8,128)(2,1)} %shard_map.73) | data formatting | bytes 524288
